TPU v7x, 32 devices: a whole 2x2x4 slice. The times are simulated.
32 devices in a mesh: row: 8 (over z, y), col: 4 (over x, core).
Axes of the slice: x: 2, y: 2, z: 4, core: 2. Of those that a mesh axis runs over, the one named last changes fastest.
Arguments:
- tensor_ri: bfloat16 [8, 8, 4, 128, 1152], P('row', None, 'col'), may hold values from -6 to 6
- block_mask: int32 [8, 4, 9], P('row', 'col'), may hold values 0 or 1
- green_virt: bfloat16 [8, 4, 128, 3200], P('row', 'col'), may hold values from -0.1875 to 0.1875
- green_occ: bfloat16 [8, 4, 128, 128], P('row', 'col'), may hold values from -0.5 to 0.5
Outputs:
- response: float32 [8, 8], replicated
All inputs are finite; a program needn't handle non-finite values. No bound on the sum of `block_mask` on one device may be relied on, other than what follows from the above.
Results may differ from a plain program's by a relative error of at most 0.0044.
Values may be sent and summed in bfloat16 or wider, within the bound.
A program may use at most 192 MiB of HBM per device.

v0:
```python
import math
import jax
import jax.numpy as jnp
from jax import lax
from jax.sharding import PartitionSpec as P


def extended(cells, sides, width):
    for axis, dim in sides:
        count = lax.axis_size(axis)
        ends = count - 1
        head = lax.slice_in_dim(cells, 0, width, axis=dim)
        tail = lax.slice_in_dim(cells, cells.shape[dim] - width, cells.shape[dim], axis=dim)
        cells = jnp.concatenate(
            [
                lax.ppermute(tail, axis, [(i, (i + 1) % count) for i in range(ends)]),
                cells,
                lax.ppermute(head, axis, [((i + 1) % count, i) for i in range(ends)]),
            ],
            axis=dim,
        )
    return cells


def window_of(band, src_row, src_col, block_width):
    grid_band = band.reshape(block_width, 5, 5, block_width)
    picked = grid_band[:, 2 - src_row : 5 - src_row, 2 - src_col : 5 - src_col, :]
    return picked.reshape(block_width, 9 * block_width)


def per_device(tensor_ri, block_mask, green_virt, green_occ):
    row_count = lax.axis_size("row")
    col_count = lax.axis_size("col")
    block_width = green_occ.shape[-1]
    pair_width = tensor_ri.shape[-1]
    occ_block = green_occ[0, 0]
    regrouped = lax.all_to_all(tensor_ri, "row", split_axis=1, concat_axis=0, tiled=True)
    occ_applied = jnp.einsum(
        "ji,pabiw->pabjw", occ_block, regrouped, preferred_element_type=jnp.float32
    ).astype(jnp.bfloat16)
    rows_all = regrouped.shape[0]
    regrouped = regrouped.reshape(rows_all, block_width, pair_width)
    occ_applied = occ_applied.reshape(rows_all, block_width, pair_width)
    grid_row = lax.axis_index("row")
    grid_col = lax.axis_index("col")
    slots = jnp.arange(9, dtype=jnp.int32)
    near_row = grid_row + slots // 3 - 1
    near_col = grid_col + slots % 3 - 1
    usable = (
        (block_mask[0, 0] == 1)
        & (near_row >= 0)
        & (near_row < row_count)
        & (near_col >= 0)
        & (near_col < col_count)
    )
    kept_slots = jnp.repeat(usable.astype(jnp.bfloat16), block_width)
    regrouped = regrouped * kept_slots
    occ_applied = occ_applied * kept_slots
    windows = []
    rim_blocks = extended(green_virt, (("row", 0), ("col", 1)), 1)
    for source in range(9):
        src_row, src_col = (source // 3, source % 3)
        windows.append(window_of(rim_blocks[src_row, src_col], src_row, src_col, block_width))
    flat_rows = regrouped.reshape(rows_all * block_width, pair_width)
    half_sum = jnp.zeros((rows_all * block_width, pair_width), jnp.float32)
    for source in range(9):
        tile = flat_rows[:, source * block_width : (source + 1) * block_width]
        half_sum = half_sum + jnp.dot(tile, windows[source], preferred_element_type=jnp.float32)
    half_done = half_sum.astype(jnp.bfloat16).reshape(rows_all, block_width * pair_width)
    occ_flat = occ_applied.reshape(rows_all, block_width * pair_width)
    partial_value = lax.dot_general(
        half_done, occ_flat, (((1,), (1,)), ((), ())), preferred_element_type=jnp.float32
    )
    total_basis = block_width * row_count * col_count
    response = lax.psum(partial_value, ("row", "col"))
    return response * (1.0 / math.sqrt(total_basis * 9 * block_width))


def solution(mesh):
    return jax.shard_map(
        per_device,
        mesh=mesh,
        in_specs=(
            P("row", None, "col", None, None),
            P("row", "col", None),
            P("row", "col", None, None),
            P("row", "col", None, None),
        ),
        out_specs=P(),
        check_vma=False,
    )
```

profile of v0, /device:TPU:10, one launch (start us, length us, event | category | flops | bytes accessed | tf_op | source)
XLA Modules:
  0.0 181.1 jit_solution(1390845295951888833)
XLA Ops:
  0.0 1.7 copy.15
  1.7 3.4 %collective-permute-start.1 = (bf16[1,1,128,3200]{2,3,1,0:T(8,128)(2,1)S(1)}, bf16[1,1,128,3200]{2,3,1,0:T(8,128)(2,1)S(1)}, u32[]{:S(2)}, u32[]{:S(2)}) collective-permute-start(bf16[1,1,128,3200]{2,3,1,0:T(8,128)(2,1)S(1)} %copy.15), channel_id=1, source_target_pairs={{4,0},{8,4},{12,8},{16,12},{20,16},{24,20},{28,24},{5,1},{9,5},{13... | collective-permute-start | bytes 2457608 | tf_op jit(solution)/shard_map/ppermute | solution.py:18
  5.2 2.5 %collective-permute-start = (bf16[1,1,128,3200]{2,3,1,0:T(8,128)(2,1)S(1)}, bf16[1,1,128,3200]{2,3,1,0:T(8,128)(2,1)S(1)}, u32[]{:S(2)}, u32[]{:S(2)}) collective-permute-start(bf16[1,1,128,3200]{2,3,1,0:T(8,128)(2,1)S(1)} %copy.15), channel_id=1, source_target_pairs={{0,4},{4,8},{8,12},{12,16},{16,20},{20,24},{24,28},{1,5},{5,9},{9,... | collective-permute-start | bytes 2457608 | tf_op jit(solution)/shard_map/ppermute | solution.py:16
  7.7 33.6 %collective-permute-done.1 = bf16[1,1,128,3200]{2,3,1,0:T(8,128)(2,1)S(1)} collective-permute-done((bf16[1,1,128,3200]{2,3,1,0:T(8,128)(2,1)S(1)}, bf16[1,1,128,3200]{2,3,1,0:T(8,128)(2,1)S(1)}, u32[]{:S(2)}, u32[]{:S(2)}) %collective-permute-start.1) | collective-permute-done | bytes 819232 | tf_op jit(solution)/shard_map/ppermute | solution.py:18
  42.2 1.7 pad_maximum_fusion
  43.9 1.9 %collective-permute-start.3 = (bf16[3,1,128,3200]{2,3,1,0:T(8,128)(2,1)}, bf16[3,1,128,3200]{2,3,1,0:T(8,128)(2,1)}, u32[]{:S(2)}, u32[]{:S(2)}) collective-permute-start(bf16[3,1,128,3200]{2,3,1,0:T(8,128)(2,1)} %pad_maximum_fusion), channel_id=1, source_target_pairs={{1,0},{2,1},{3,2},{5,4},{6,5},{7,6},{9,8},{10,9},{11,10},{13,12},{... | collective-permute-start | bytes 7372808 | tf_op jit(solution)/shard_map/ppermute | solution.py:18
  45.9 2.6 %copy.13 = bf16[1,8,1,128,1152]{3,4,2,0,1:T(8,128)(2,1)} copy(bf16[1,8,1,128,1152]{4,3,2,1,0:T(8,128)(2,1)S(1)} %copy-done.3) | data formatting | bytes 4718592 | tf_op args[0]
  48.4 5.5 %all-to-all-start = ((bf16[1,8,1,128,1152]{3,4,2,0,1:T(8,128)(2,1)}), bf16[1,8,1,128,1152]{3,4,2,0,1:T(8,128)(2,1)S(1)}, u32[]{:S(2)}, u32[]{:S(2)}) async-start(bf16[1,8,1,128,1152]{3,4,2,0,1:T(8,128)(2,1)} %copy.13), calls=%async_computation | async-start | bytes 4718592 | tf_op jit(solution)/shard_map/all_to_all | solution.py:37
  54.0 3.2 %collective-permute-start.2 = (bf16[3,1,128,3200]{2,3,1,0:T(8,128)(2,1)}, bf16[3,1,128,3200]{2,3,1,0:T(8,128)(2,1)}, u32[]{:S(2)}, u32[]{:S(2)}) collective-permute-start(bf16[3,1,128,3200]{2,3,1,0:T(8,128)(2,1)} %pad_maximum_fusion), channel_id=1, source_target_pairs={{0,1},{1,2},{2,3},{4,5},{5,6},{6,7},{8,9},{9,10},{10,11},{12,13},{... | collective-permute-start | bytes 7372808 | tf_op jit(solution)/shard_map/ppermute | solution.py:16
  58.3 1.7 slice.100
  60.0 13.6 %collective-permute-done.3 = bf16[3,1,128,3200]{2,3,1,0:T(8,128)(2,1)} collective-permute-done((bf16[3,1,128,3200]{2,3,1,0:T(8,128)(2,1)}, bf16[3,1,128,3200]{2,3,1,0:T(8,128)(2,1)}, u32[]{:S(2)}, u32[]{:S(2)}) %collective-permute-start.3) | collective-permute-done | bytes 2457632 | tf_op jit(solution)/shard_map/ppermute | solution.py:18
  73.6 1.8 fusion.27
  76.9 8.6 %collective-permute-done.2 = bf16[3,1,128,3200]{2,3,1,0:T(8,128)(2,1)} collective-permute-done((bf16[3,1,128,3200]{2,3,1,0:T(8,128)(2,1)}, bf16[3,1,128,3200]{2,3,1,0:T(8,128)(2,1)}, u32[]{:S(2)}, u32[]{:S(2)}) %collective-permute-start.2) | collective-permute-done | bytes 2457632 | tf_op jit(solution)/shard_map/ppermute | solution.py:16
  85.5 1.8 fusion.26
  89.5 17.2 %all-to-all-done = bf16[1,8,1,128,1152]{3,4,2,0,1:T(8,128)(2,1)S(1)} async-done(((bf16[1,8,1,128,1152]{3,4,2,0,1:T(8,128)(2,1)}), bf16[1,8,1,128,1152]{3,4,2,0,1:T(8,128)(2,1)S(1)}, u32[]{:S(2)}, u32[]{:S(2)}) %all-to-all-start) | async-done | bytes 2359328 | tf_op jit(solution)/shard_map/all_to_all | solution.py:37
  106.7 2.6 %copy.14 = bf16[1,8,1,128,1152]{4,3,1,2,0:T(8,128)(2,1)} copy(bf16[1,8,1,128,1152]{3,4,2,0,1:T(8,128)(2,1)S(1)} %all-to-all-done) | data formatting | bytes 4718592 | tf_op jit(solution)/shard_map/all_to_all | solution.py:37
  109.3 3.3 %bitcast_multiply_fusion = bf16[1024,1152]{1,0:T(8,128)(2,1)} fusion(bf16[1,8,1,128,1152]{4,3,1,2,0:T(8,128)(2,1)} %copy.14, bf16[1152]{0:T(1024)(128)(2,1)S(1)} %broadcast_bitcast_fusion), kind=kLoop, calls=%fused_computation.15 | loop fusion | flops 1179648 | bytes 4720896 | tf_op jit(solution)/shard_map/mul | solution.py:57
  112.6 2.2 %fusion.4 = bf16[8,1,1,128,1152]{3,4,0,2,1:T(8,128)(2,1)} fusion(bf16[1,8,1,128,1152]{3,4,2,0,1:T(8,128)(2,1)S(1)} %all-to-all-done, bf16[1152]{0:T(1024)(128)(2,1)S(1)} %broadcast_bitcast_fusion, bf16[1,1,128,128]{3,2,1,0:T(8,128)(2,1)S(1)} %copy-done), kind=kOutput, calls=%fused_computation.12 | convolution fusion | flops 304349184 | bytes 4753664 | tf_op jit(solution)/shard_map/ji,pabiw->pabjw/dot_general | solution.py:38
  114.8 4.3 %copy.19 = bf16[8,1,1,128,1152]{4,3,0,2,1:T(8,128)(2,1)} copy(bf16[8,1,1,128,1152]{3,4,0,2,1:T(8,128)(2,1)} %fusion.4) | data formatting | bytes 4718592 | tf_op jit(solution)/shard_map/mul | solution.py:58
  119.1 3.1 %copy.20 = bf16[1,8,128,1152]{3,1,2,0:T(8,128)(2,1)S(1)} copy(bf16[1,8,128,1152]{3,2,1,0:T(8,128)(2,1)} %bitcast.64) | data formatting | bytes 4718592
  129.5 2.2 %fusion.1 = bf16[1024,1152]{1,0:T(8,128)(2,1)} fusion(f32[1024,1152]{1,0:T(8,128)S(1)} %fusion.6, f32[1024,1152]{1,0:T(8,128)S(1)} %convolution_add_fusion.1, bf16[128,1152]{0,1:T(8,128)(2,1)S(1)} %bitcast.74, bf16[1024,1152]{1,0:T(8,128)(2,1)S(1)} %copy-done.2), kind=kOutput, calls=%fused_computation.8 | convolution fusion | flops 305528832 | bytes 12353536 | tf_op jit(solution)/shard_map/dot_general | solution.py:68
  131.7 4.1 %reshape.69 = bf16[8,147456]{1,0:T(8,128)(2,1)} reshape(bf16[1024,1152]{1,0:T(8,128)(2,1)} %fusion.1) | data formatting | bytes 4718592 | tf_op jit(solution)/shard_map/reshape | solution.py:69
  135.9 3.3 %fusion.28 = f32[8,8]{1,0:T(8,128)S(1)} fusion(bf16[8,147456]{1,0:T(8,128)(2,1)} %reshape.69, bf16[8,147456]{1,0:T(8,128)(2,1)S(1)} %bitcast.63), kind=kOutput, calls=%fused_computation.46 | convolution fusion | flops 18874368 | bytes 4718848 | tf_op jit(solution)/shard_map/dot_general | solution.py:71
  139.1 41.3 %psum.7 = f32[8,8]{1,0:T(8,128)S(1)} all-reduce(f32[8,8]{1,0:T(8,128)S(1)} %fusion.28), channel_id=1, replica_groups=mesh['row'=8,'col'=4] {'row','col'}, use_global_device_ids=true, to_apply=%region_0.1 | all-reduce | flops 64 | bytes 512 | tf_op jit(solution)/shard_map/psum | solution.py:75
  (46 shorter events, 13.5 us)
Async XLA Ops:
  0.0 112.6 %copy-start = (bf16[1,1,128,128]{3,2,1,0:T(8,128)(2,1)S(1)}, bf16[1,1,128,128]{3,2,1,0:T(8,128)(2,1)}, u32[]{:S(2)}) copy-start(bf16[1,1,128,128]{3,2,1,0:T(8,128)(2,1)} %param.7) | copy-start | bytes 98308
  1.7 44.1 %copy-start.3 = (bf16[1,8,1,128,1152]{4,3,2,1,0:T(8,128)(2,1)S(1)}, bf16[1,8,1,128,1152]{4,3,2,1,0:T(8,128)(2,1)}, u32[]{:S(2)}) copy-start(bf16[1,8,1,128,1152]{4,3,2,1,0:T(8,128)(2,1)} %param.4) | copy-start | bytes 7077892
  1.7 39.6 %collective-permute-start.1 = (bf16[1,1,128,3200]{2,3,1,0:T(8,128)(2,1)S(1)}, bf16[1,1,128,3200]{2,3,1,0:T(8,128)(2,1)S(1)}, u32[]{:S(2)}, u32[]{:S(2)}) collective-permute-start(bf16[1,1,128,3200]{2,3,1,0:T(8,128)(2,1)S(1)} %copy.15), channel_id=1, source_target_pairs={{4,0},{8,4},{12,8},{16,12},{20,16},{24,20},{28,24},{5,1},{9,5},{13... | collective-permute-start | bytes 2457608 | tf_op jit(solution)/shard_map/ppermute | solution.py:18
  5.2 36.1 %collective-permute-start = (bf16[1,1,128,3200]{2,3,1,0:T(8,128)(2,1)S(1)}, bf16[1,1,128,3200]{2,3,1,0:T(8,128)(2,1)S(1)}, u32[]{:S(2)}, u32[]{:S(2)}) collective-permute-start(bf16[1,1,128,3200]{2,3,1,0:T(8,128)(2,1)S(1)} %copy.15), channel_id=1, source_target_pairs={{0,4},{4,8},{8,12},{12,16},{16,20},{20,24},{24,28},{1,5},{5,9},{9,... | collective-permute-start | bytes 2457608 | tf_op jit(solution)/shard_map/ppermute | solution.py:16
  41.3 0.9 copy-start.4
  42.2 1.7 copy-start.5
  43.9 29.6 %collective-permute-start.3 = (bf16[3,1,128,3200]{2,3,1,0:T(8,128)(2,1)}, bf16[3,1,128,3200]{2,3,1,0:T(8,128)(2,1)}, u32[]{:S(2)}, u32[]{:S(2)}) collective-permute-start(bf16[3,1,128,3200]{2,3,1,0:T(8,128)(2,1)} %pad_maximum_fusion), channel_id=1, source_target_pairs={{1,0},{2,1},{3,2},{5,4},{6,5},{7,6},{9,8},{10,9},{11,10},{13,12},{... | collective-permute-start | bytes 7372808 | tf_op jit(solution)/shard_map/ppermute | solution.py:18
  48.4 8.8 %copy-start.12 = (s32[1,1,9]{2,1,0:T(1,128)S(1)}, s32[1,1,9]{2,1,0:T(1,128)}, u32[]{:S(2)}) copy-start(s32[1,1,9]{2,1,0:T(1,128)} %param.5) | copy-start | bytes 112
  48.4 58.3 %all-to-all-start = ((bf16[1,8,1,128,1152]{3,4,2,0,1:T(8,128)(2,1)}), bf16[1,8,1,128,1152]{3,4,2,0,1:T(8,128)(2,1)S(1)}, u32[]{:S(2)}, u32[]{:S(2)}) async-start(bf16[1,8,1,128,1152]{3,4,2,0,1:T(8,128)(2,1)} %copy.13), calls=%async_computation | async-start | bytes 4718592 | tf_op jit(solution)/shard_map/all_to_all | solution.py:37
  54.0 31.5 %collective-permute-start.2 = (bf16[3,1,128,3200]{2,3,1,0:T(8,128)(2,1)}, bf16[3,1,128,3200]{2,3,1,0:T(8,128)(2,1)}, u32[]{:S(2)}, u32[]{:S(2)}) collective-permute-start(bf16[3,1,128,3200]{2,3,1,0:T(8,128)(2,1)} %pad_maximum_fusion), channel_id=1, source_target_pairs={{0,1},{1,2},{2,3},{4,5},{5,6},{6,7},{8,9},{9,10},{10,11},{12,13},{... | collective-permute-start | bytes 7372808 | tf_op jit(solution)/shard_map/ppermute | solution.py:16
  119.1 3.1 %copy-start.2 = (bf16[1024,1152]{1,0:T(8,128)(2,1)S(1)}, bf16[1024,1152]{1,0:T(8,128)(2,1)}, u32[]{:S(2)}) copy-start(bf16[1024,1152]{1,0:T(8,128)(2,1)} %bitcast_multiply_fusion) | copy-start | bytes 7077892
  119.1 3.1 %copy-start.9 = (bf16[128,3,3,128]{0,3,2,1:T(8,128)(2,1)S(1)}, bf16[128,3,3,128]{0,3,2,1:T(8,128)(2,1)}, u32[]{:S(2)}) copy-start(bf16[128,3,3,128]{0,3,2,1:T(8,128)(2,1)} %slice.119) | copy-start | bytes 884740
  122.3 1.0 copy-start.6
  123.3 1.0 copy-start.11
  124.2 1.0 copy-start.8
  125.2 1.0 copy-start.10
  127.7 1.0 copy-start.7
  131.7 49.4 %copy-start.1 = (bf16[1,1,128,128]{3,2,1,0:T(8,128)(2,1)S(1)}, bf16[1,1,128,128]{3,2,1,0:T(8,128)(2,1)}, u32[]{:S(2)}) copy-start(bf16[1,1,128,128]{3,2,1,0:T(8,128)(2,1)} %param.7) | copy-start | bytes 98308
where the time goes:
time: 182 us; the launch traced here: 181 us
  waiting for transfers between devices  72.9 us (40%)
  blocking collectives  41.3 us (23%)
  local copies, waits for them, and re-layouts  30.4 us (17%)
  starting transfers between devices  16.6 us (9%)
  matrix products  14 us (8%)
  other arithmetic  5.65 us (3%)
    ppermute x2, waiting for transfers between devices, extended(): lax.ppermute(head, axis, [((i + 1) % count, i) for i in range(ends)])  47.1 us
    psum x1, blocking collectives, per_device(): response = lax.psum(partial_value, ('row', 'col'))  41.3 us
    all_to_all x1, waiting for transfers between devices, per_device(): lax.all_to_all(tensor_ri, 'row', split_axis=1, concat_axis=0, tiled=True)  17.2 us
    unnamed x29, local copies, waits for them, and re-layouts  9.19 us
    ppermute x2, waiting for transfers between devices, extended(): lax.ppermute(tail, axis, [(i, (i + 1) % count) for i in range(ends)])  8.6 us
    dot_general x9, matrix products, per_device(): jnp.dot(tile, windows[source], preferred_element_type=jnp.float32)  8.5 us
    slice x9, local copies, waits for them, and re-layouts, window_of(): picked = grid_band[:, 2 - src_row:5 - src_row, 2 - src_col:5 - src_col, :]  6.45 us
    ppermute x2, starting transfers between devices, extended(): lax.ppermute(tail, axis, [(i, (i + 1) % count) for i in range(ends)])  5.74 us
  transfers between devices with their start and end apart: 5, of which 4 were waited for; matrix products, arithmetic and copies ran while one was open for 7% of the time, Pallas kernels for 0%

commit v1 on v0

--- a/solution.py
+++ b/solution.py
@@ -34,7 +34,10 @@
     block_width = green_occ.shape[-1]
     pair_width = tensor_ri.shape[-1]
     occ_block = green_occ[0, 0]
-    regrouped = lax.all_to_all(tensor_ri, "row", split_axis=1, concat_axis=0, tiled=True)
+    regrouped = jnp.concatenate(
+        lax.all_to_all(jnp.stack(jnp.split(tensor_ri, lax.axis_size("row"), axis=1)), "row", 0, 0),
+        axis=0,
+    )
     occ_applied = jnp.einsum(
         "ji,pabiw->pabjw", occ_block, regrouped, preferred_element_type=jnp.float32
     ).astype(jnp.bfloat16)

time: 182 us -> 180 us (0.989)
  waiting for transfers between devices: 72.9 us -> 49.1 us
  local copies, waits for them, and re-layouts: 30.4 us -> 51.4 us
    ppermute x2, waiting for transfers between devices: 47.1 us -> 24.4 us  [extended(): lax.ppermute(head, axis, [((i + 1) % count, i) for i in range(ends)])]
    unnamed x29 -> x49, local copies, waits for them, and re-layouts: 9.19 us -> 26.7 us
    split x0 -> x1, local copies, waits for them, and re-layouts: none -> 2.75 us  [per_device(): jnp.split(tensor_ri, lax.axis_size('row'), axis=1)]
  transfers between devices with their start and end apart: 5 -> 5, of which waited for: 4 -> 4; matrix products, arithmetic and copies ran while one was open for 7% -> 19% of each run, Pallas kernels for 0% -> 0%
where the time goes in v1:
time: 180 us; the launch traced here: 179 us
  local copies, waits for them, and re-layouts  51.4 us (29%)
  waiting for transfers between devices  49.1 us (27%)
  blocking collectives  41.4 us (23%)
  starting transfers between devices  17.3 us (10%)
  matrix products  14 us (8%)
  other arithmetic  5.85 us (3%)
    psum x1, blocking collectives, per_device(): response = lax.psum(partial_value, ('row', 'col'))  41.4 us
    unnamed x49, local copies, waits for them, and re-layouts  26.7 us
    ppermute x2, waiting for transfers between devices, extended(): lax.ppermute(head, axis, [((i + 1) % count, i) for i in range(ends)])  24.4 us
    all_to_all x1, waiting for transfers between devices, per_device(): lax.all_to_all(jnp.stack(jnp.split(tensor_ri, lax.axis_size('row'), axis=...  17.2 us
    dot_general x9, matrix products, per_device(): jnp.dot(tile, windows[source], preferred_element_type=jnp.float32)  8.51 us
    ppermute x2, waiting for transfers between devices, extended(): lax.ppermute(tail, axis, [(i, (i + 1) % count) for i in range(ends)])  7.46 us
    slice x9, local copies, waits for them, and re-layouts, window_of(): picked = grid_band[:, 2 - src_row:5 - src_row, 2 - src_col:5 - src_col, :]  6.44 us
    all_to_all x1, starting transfers between devices, per_device(): lax.all_to_all(jnp.stack(jnp.split(tensor_ri, lax.axis_size('row'), axis=...  6.22 us
  transfers between devices with their start and end apart: 5, of which 4 were waited for; matrix products, arithmetic and copies ran while one was open for 19% of the time, Pallas kernels for 0%

profile of v1, /device:TPU:10, one launch (start us, length us, event | category | flops | bytes accessed | tf_op | source)
XLA Modules:
  0.0 179.3 jit_solution(2618375892979488756)
XLA Ops:
  1.7 3.3 %collective-permute-start.1 = (bf16[1,1,128,3200]{2,3,1,0:T(8,128)(2,1)S(1)}, bf16[1,1,128,3200]{2,3,1,0:T(8,128)(2,1)S(1)}, u32[]{:S(2)}, u32[]{:S(2)}) collective-permute-start(bf16[1,1,128,3200]{2,3,1,0:T(8,128)(2,1)S(1)} %copy.36), channel_id=1, source_target_pairs={{4,0},{8,4},{12,8},{16,12},{20,16},{24,20},{28,24},{5,1},{9,5},{13... | collective-permute-start | bytes 2457608 | tf_op jit(solution)/shard_map/ppermute | solution.py:18
  5.0 2.5 %collective-permute-start = (bf16[1,1,128,3200]{2,3,1,0:T(8,128)(2,1)S(1)}, bf16[1,1,128,3200]{2,3,1,0:T(8,128)(2,1)S(1)}, u32[]{:S(2)}, u32[]{:S(2)}) collective-permute-start(bf16[1,1,128,3200]{2,3,1,0:T(8,128)(2,1)S(1)} %copy.36), channel_id=1, source_target_pairs={{0,4},{4,8},{8,12},{12,16},{16,20},{20,24},{24,28},{1,5},{5,9},{9,... | collective-permute-start | bytes 2457608 | tf_op jit(solution)/shard_map/ppermute | solution.py:16
  7.6 2.7 %fusion.28 = (bf16[1,1,1,128,1152]{4,3,2,1,0:T(8,128)(2,1)}, bf16[1,1,1,128,1152]{4,3,2,1,0:T(8,128)(2,1)}, bf16[1,1,1,128,1152]{4,3,2,1,0:T(8,128)(2,1)}, bf16[...) fusion(bf16[1,8,1,128,1152]{4,3,2,1,0:T(8,128)(2,1)} %param.4), kind=kLoop, calls=%fused_computation.54 | loop fusion | bytes 4718592 | tf_op jit(solution)/shard_map/split | solution.py:38
  12.2 1.8 %copy.47 = bf16[1,1,1,128,1152]{3,4,2,1,0:T(8,128)(2,1)} copy(bf16[1,1,1,128,1152]{4,3,2,1,0:T(8,128)(2,1)} %get-tuple-element.12) | data formatting | bytes 589824
  14.0 1.8 %copy.46 = bf16[1,1,1,128,1152]{3,4,2,1,0:T(8,128)(2,1)} copy(bf16[1,1,1,128,1152]{4,3,2,1,0:T(8,128)(2,1)} %get-tuple-element.13) | data formatting | bytes 589824
  15.8 1.8 %copy.45 = bf16[1,1,1,128,1152]{3,4,2,1,0:T(8,128)(2,1)} copy(bf16[1,1,1,128,1152]{4,3,2,1,0:T(8,128)(2,1)} %get-tuple-element.14) | data formatting | bytes 589824
  17.7 1.8 %copy.44 = bf16[1,1,1,128,1152]{3,4,2,1,0:T(8,128)(2,1)} copy(bf16[1,1,1,128,1152]{4,3,2,1,0:T(8,128)(2,1)} %get-tuple-element.15) | data formatting | bytes 589824
  31.3 9.8 %collective-permute-done.1 = bf16[1,1,128,3200]{2,3,1,0:T(8,128)(2,1)S(1)} collective-permute-done((bf16[1,1,128,3200]{2,3,1,0:T(8,128)(2,1)S(1)}, bf16[1,1,128,3200]{2,3,1,0:T(8,128)(2,1)S(1)}, u32[]{:S(2)}, u32[]{:S(2)}) %collective-permute-start.1) | collective-permute-done | bytes 819232 | tf_op jit(solution)/shard_map/ppermute | solution.py:18
  41.2 1.9 %pad_maximum_fusion = bf16[3,1,128,3200]{2,3,1,0:T(8,128)(2,1)} fusion(bf16[1,1,128,3200]{2,3,1,0:T(8,128)(2,1)S(1)} %collective-permute-done.1, bf16[1,1,128,3200]{2,3,1,0:T(8,128)(2,1)S(1)} %copy.36, bf16[1,1,128,3200]{2,3,1,0:T(8,128)(2,1)S(1)} %collective-permute-done), kind=kLoop, calls=%fused_computation.13 | loop fusion | flops 2457600 | bytes 4915200 | tf_op jit(solution)/shard_map/concatenate | solution.py:14
  43.1 1.9 %collective-permute-start.3 = (bf16[3,1,128,3200]{2,3,1,0:T(8,128)(2,1)}, bf16[3,1,128,3200]{2,3,1,0:T(8,128)(2,1)}, u32[]{:S(2)}, u32[]{:S(2)}) collective-permute-start(bf16[3,1,128,3200]{2,3,1,0:T(8,128)(2,1)} %pad_maximum_fusion), channel_id=1, source_target_pairs={{1,0},{2,1},{3,2},{5,4},{6,5},{7,6},{9,8},{10,9},{11,10},{13,12},{... | collective-permute-start | bytes 7372808 | tf_op jit(solution)/shard_map/ppermute | solution.py:18
  45.8 6.2 %all-to-all-start = ((bf16[8,1,1,1,128,1152]{4,5,3,2,1,0:T(8,128)(2,1)}), bf16[8,1,1,1,128,1152]{4,5,3,2,1,0:T(8,128)(2,1)S(1)}, u32[]{:S(2)}, u32[]{:S(2)}) async-start(bf16[8,1,1,1,128,1152]{4,5,3,2,1,0:T(8,128)(2,1)} %bitcast_dynamic-update-slice_fusion), calls=%async_computation | async-start | bytes 4718592 | tf_op jit(solution)/shard_map/all_to_all | solution.py:38
  52.0 3.3 %collective-permute-start.2 = (bf16[3,1,128,3200]{2,3,1,0:T(8,128)(2,1)}, bf16[3,1,128,3200]{2,3,1,0:T(8,128)(2,1)}, u32[]{:S(2)}, u32[]{:S(2)}) collective-permute-start(bf16[3,1,128,3200]{2,3,1,0:T(8,128)(2,1)} %pad_maximum_fusion), channel_id=1, source_target_pairs={{0,1},{1,2},{2,3},{4,5},{5,6},{6,7},{8,9},{9,10},{10,11},{12,13},{... | collective-permute-start | bytes 7372808 | tf_op jit(solution)/shard_map/ppermute | solution.py:16
  58.2 14.6 %collective-permute-done.3 = bf16[3,1,128,3200]{2,3,1,0:T(8,128)(2,1)} collective-permute-done((bf16[3,1,128,3200]{2,3,1,0:T(8,128)(2,1)}, bf16[3,1,128,3200]{2,3,1,0:T(8,128)(2,1)}, u32[]{:S(2)}, u32[]{:S(2)}) %collective-permute-start.3) | collective-permute-done | bytes 2457632 | tf_op jit(solution)/shard_map/ppermute | solution.py:18
  76.1 7.5 %collective-permute-done.2 = bf16[3,1,128,3200]{2,3,1,0:T(8,128)(2,1)} collective-permute-done((bf16[3,1,128,3200]{2,3,1,0:T(8,128)(2,1)}, bf16[3,1,128,3200]{2,3,1,0:T(8,128)(2,1)}, u32[]{:S(2)}, u32[]{:S(2)}) %collective-permute-start.2) | collective-permute-done | bytes 2457632 | tf_op jit(solution)/shard_map/ppermute | solution.py:16
  87.5 17.2 %all-to-all-done = bf16[8,1,1,1,128,1152]{4,5,3,2,1,0:T(8,128)(2,1)S(1)} async-done(((bf16[8,1,1,1,128,1152]{4,5,3,2,1,0:T(8,128)(2,1)}), bf16[8,1,1,1,128,1152]{4,5,3,2,1,0:T(8,128)(2,1)S(1)}, u32[]{:S(2)}, u32[]{:S(2)}) %all-to-all-start) | async-done | bytes 2359328 | tf_op jit(solution)/shard_map/all_to_all | solution.py:38
  104.8 2.6 %copy.35 = bf16[8,1,1,1,128,1152]{5,4,0,3,2,1:T(8,128)(2,1)} copy(bf16[8,1,1,1,128,1152]{4,5,3,2,1,0:T(8,128)(2,1)S(1)} %all-to-all-done) | data formatting | bytes 4718592 | tf_op jit(solution)/shard_map/all_to_all | solution.py:38
  107.3 3.3 %bitcast_multiply_fusion = bf16[1024,1152]{1,0:T(8,128)(2,1)} fusion(bf16[8,1,1,1,128,1152]{5,4,0,3,2,1:T(8,128)(2,1)} %copy.35, bf16[1152]{0:T(1024)(128)(2,1)S(1)} %broadcast_bitcast_fusion), kind=kLoop, calls=%fused_computation.15 | loop fusion | flops 1179648 | bytes 4720896 | tf_op jit(solution)/shard_map/mul | solution.py:60
  110.6 2.2 %fusion.4 = bf16[8,1,1,128,1152]{3,4,0,2,1:T(8,128)(2,1)} fusion(bf16[8,1,1,1,128,1152]{4,5,3,2,1,0:T(8,128)(2,1)S(1)} %all-to-all-done, bf16[1152]{0:T(1024)(128)(2,1)S(1)} %broadcast_bitcast_fusion, bf16[1,1,128,128]{3,2,1,0:T(8,128)(2,1)S(1)} %copy-done), kind=kOutput, calls=%fused_computation.12 | convolution fusion | flops 304349184 | bytes 4753664 | tf_op jit(solution)/shard_map/ji,pabiw->pabjw/dot_general | solution.py:41
  112.9 4.3 %copy.40 = bf16[8,1,1,128,1152]{4,3,0,2,1:T(8,128)(2,1)} copy(bf16[8,1,1,128,1152]{3,4,0,2,1:T(8,128)(2,1)} %fusion.4) | data formatting | bytes 4718592 | tf_op jit(solution)/shard_map/mul | solution.py:61
  117.2 3.1 %copy.49 = bf16[1,8,128,1152]{3,1,2,0:T(8,128)(2,1)S(1)} copy(bf16[1,8,128,1152]{3,2,1,0:T(8,128)(2,1)} %bitcast.80) | data formatting | bytes 4718592
  127.6 2.2 %fusion.1 = bf16[1024,1152]{1,0:T(8,128)(2,1)} fusion(f32[1024,1152]{1,0:T(8,128)S(1)} %fusion.6, f32[1024,1152]{1,0:T(8,128)S(1)} %convolution_add_fusion.1, bf16[128,1152]{0,1:T(8,128)(2,1)S(1)} %bitcast.90, bf16[1024,1152]{1,0:T(8,128)(2,1)S(1)} %copy-done.2), kind=kOutput, calls=%fused_computation.8 | convolution fusion | flops 305528832 | bytes 12353536 | tf_op jit(solution)/shard_map/dot_general | solution.py:71
  129.8 4.2 %reshape.61 = bf16[8,147456]{1,0:T(8,128)(2,1)} reshape(bf16[1024,1152]{1,0:T(8,128)(2,1)} %fusion.1) | data formatting | bytes 4718592 | tf_op jit(solution)/shard_map/reshape | solution.py:72
  134.0 3.3 %fusion.29 = f32[8,8]{1,0:T(8,128)S(1)} fusion(bf16[8,147456]{1,0:T(8,128)(2,1)} %reshape.61, bf16[8,147456]{1,0:T(8,128)(2,1)S(1)} %bitcast.79), kind=kOutput, calls=%fused_computation.55 | convolution fusion | flops 18874368 | bytes 4718848 | tf_op jit(solution)/shard_map/dot_general | solution.py:74
  137.3 41.4 %psum.7 = f32[8,8]{1,0:T(8,128)S(1)} all-reduce(f32[8,8]{1,0:T(8,128)S(1)} %fusion.29), channel_id=1, replica_groups=mesh['row'=8,'col'=4] {'row','col'}, use_global_device_ids=true, to_apply=%region_0.1 | all-reduce | flops 64 | bytes 512 | tf_op jit(solution)/shard_map/psum | solution.py:78
  (68 shorter events, 34.0 us)
Async XLA Ops:
  0.0 110.6 %copy-start = (bf16[1,1,128,128]{3,2,1,0:T(8,128)(2,1)S(1)}, bf16[1,1,128,128]{3,2,1,0:T(8,128)(2,1)}, u32[]{:S(2)}) copy-start(bf16[1,1,128,128]{3,2,1,0:T(8,128)(2,1)} %param.7) | copy-start | bytes 98308
  1.7 39.4 %collective-permute-start.1 = (bf16[1,1,128,3200]{2,3,1,0:T(8,128)(2,1)S(1)}, bf16[1,1,128,3200]{2,3,1,0:T(8,128)(2,1)S(1)}, u32[]{:S(2)}, u32[]{:S(2)}) collective-permute-start(bf16[1,1,128,3200]{2,3,1,0:T(8,128)(2,1)S(1)} %copy.36), channel_id=1, source_target_pairs={{4,0},{8,4},{12,8},{16,12},{20,16},{24,20},{28,24},{5,1},{9,5},{13... | collective-permute-start | bytes 2457608 | tf_op jit(solution)/shard_map/ppermute | solution.py:18
  5.0 36.1 %collective-permute-start = (bf16[1,1,128,3200]{2,3,1,0:T(8,128)(2,1)S(1)}, bf16[1,1,128,3200]{2,3,1,0:T(8,128)(2,1)S(1)}, u32[]{:S(2)}, u32[]{:S(2)}) collective-permute-start(bf16[1,1,128,3200]{2,3,1,0:T(8,128)(2,1)S(1)} %copy.36), channel_id=1, source_target_pairs={{0,4},{4,8},{8,12},{12,16},{16,20},{20,24},{24,28},{1,5},{5,9},{9,... | collective-permute-start | bytes 2457608 | tf_op jit(solution)/shard_map/ppermute | solution.py:16
  20.4 10.2 %copy-start.12 = (bf16[1,1,1,128,1152]{3,4,2,1,0:T(8,128)(2,1)S(1)}, bf16[1,1,1,128,1152]{3,4,2,1,0:T(8,128)(2,1)}, u32[]{:S(2)}) copy-start(bf16[1,1,1,128,1152]{3,4,2,1,0:T(8,128)(2,1)} %copy.47) | copy-start | bytes 884740
  21.3 8.5 %copy-start.13 = (bf16[1,1,1,128,1152]{3,4,2,1,0:T(8,128)(2,1)S(1)}, bf16[1,1,1,128,1152]{3,4,2,1,0:T(8,128)(2,1)}, u32[]{:S(2)}) copy-start(bf16[1,1,1,128,1152]{3,4,2,1,0:T(8,128)(2,1)} %copy.46) | copy-start | bytes 884740
  22.2 6.9 %copy-start.14 = (bf16[1,1,1,128,1152]{3,4,2,1,0:T(8,128)(2,1)S(1)}, bf16[1,1,1,128,1152]{3,4,2,1,0:T(8,128)(2,1)}, u32[]{:S(2)}) copy-start(bf16[1,1,1,128,1152]{3,4,2,1,0:T(8,128)(2,1)} %copy.45) | copy-start | bytes 884740
  31.3 13.7 %copy-start.11 = (bf16[1,1,1,128,1152]{3,4,2,1,0:T(8,128)(2,1)S(1)}, bf16[1,1,1,128,1152]{3,4,2,1,0:T(8,128)(2,1)}, u32[]{:S(2)}) copy-start(bf16[1,1,1,128,1152]{3,4,2,1,0:T(8,128)(2,1)} %copy.48) | copy-start | bytes 884740
  41.2 1.9 %copy-start.3 = (bf16[1,1,128,3200]{2,3,1,0:T(8,128)(2,1)}, bf16[1,1,128,3200]{2,3,1,0:T(8,128)(2,1)S(1)}, u32[]{:S(2)}) copy-start(bf16[1,1,128,3200]{2,3,1,0:T(8,128)(2,1)S(1)} %collective-permute-done.1) | copy-start | bytes 2457604
  41.2 2.0 %copy-start.4 = (bf16[1,1,128,3200]{2,3,1,0:T(8,128)(2,1)}, bf16[1,1,128,3200]{2,3,1,0:T(8,128)(2,1)S(1)}, u32[]{:S(2)}) copy-start(bf16[1,1,128,3200]{2,3,1,0:T(8,128)(2,1)S(1)} %collective-permute-done) | copy-start | bytes 2457604
  43.1 29.6 %collective-permute-start.3 = (bf16[3,1,128,3200]{2,3,1,0:T(8,128)(2,1)}, bf16[3,1,128,3200]{2,3,1,0:T(8,128)(2,1)}, u32[]{:S(2)}, u32[]{:S(2)}) collective-permute-start(bf16[3,1,128,3200]{2,3,1,0:T(8,128)(2,1)} %pad_maximum_fusion), channel_id=1, source_target_pairs={{1,0},{2,1},{3,2},{5,4},{6,5},{7,6},{9,8},{10,9},{11,10},{13,12},{... | collective-permute-start | bytes 7372808 | tf_op jit(solution)/shard_map/ppermute | solution.py:18
  45.8 9.6 %copy-start.15 = (s32[1,1,9]{2,1,0:T(1,128)S(1)}, s32[1,1,9]{2,1,0:T(1,128)}, u32[]{:S(2)}) copy-start(s32[1,1,9]{2,1,0:T(1,128)} %param.5) | copy-start | bytes 112
  45.8 59.0 %all-to-all-start = ((bf16[8,1,1,1,128,1152]{4,5,3,2,1,0:T(8,128)(2,1)}), bf16[8,1,1,1,128,1152]{4,5,3,2,1,0:T(8,128)(2,1)S(1)}, u32[]{:S(2)}, u32[]{:S(2)}) async-start(bf16[8,1,1,1,128,1152]{4,5,3,2,1,0:T(8,128)(2,1)} %bitcast_dynamic-update-slice_fusion), calls=%async_computation | async-start | bytes 4718592 | tf_op jit(solution)/shard_map/all_to_all | solution.py:38
  52.0 31.5 %collective-permute-start.2 = (bf16[3,1,128,3200]{2,3,1,0:T(8,128)(2,1)}, bf16[3,1,128,3200]{2,3,1,0:T(8,128)(2,1)}, u32[]{:S(2)}, u32[]{:S(2)}) collective-permute-start(bf16[3,1,128,3200]{2,3,1,0:T(8,128)(2,1)} %pad_maximum_fusion), channel_id=1, source_target_pairs={{0,1},{1,2},{2,3},{4,5},{5,6},{6,7},{8,9},{9,10},{10,11},{12,13},{... | collective-permute-start | bytes 7372808 | tf_op jit(solution)/shard_map/ppermute | solution.py:16
  117.2 3.1 %copy-start.2 = (bf16[1024,1152]{1,0:T(8,128)(2,1)S(1)}, bf16[1024,1152]{1,0:T(8,128)(2,1)}, u32[]{:S(2)}) copy-start(bf16[1024,1152]{1,0:T(8,128)(2,1)} %bitcast_multiply_fusion) | copy-start | bytes 7077892
  117.2 3.1 %copy-start.8 = (bf16[128,3,3,128]{0,3,2,1:T(8,128)(2,1)S(1)}, bf16[128,3,3,128]{0,3,2,1:T(8,128)(2,1)}, u32[]{:S(2)}) copy-start(bf16[128,3,3,128]{0,3,2,1:T(8,128)(2,1)} %slice.119) | copy-start | bytes 884740
  120.4 1.0 copy-start.5
  121.3 1.0 copy-start.10
  122.3 1.0 copy-start.7
  123.3 1.0 copy-start.9
  125.8 1.0 copy-start.6
  134.0 45.3 %copy-start.1 = (bf16[1,1,128,128]{3,2,1,0:T(8,128)(2,1)S(1)}, bf16[1,1,128,128]{3,2,1,0:T(8,128)(2,1)}, u32[]{:S(2)}) copy-start(bf16[1,1,128,128]{3,2,1,0:T(8,128)(2,1)} %param.7) | copy-start | bytes 98308
